TPU v7x, 512 devices: a whole 4x4x16 slice. The times are simulated.
512 devices in a mesh: ctx: 64 (over x, z), head: 8 (over y, core).
Axes of the slice: x: 4, y: 4, z: 16, core: 2. Of those that a mesh axis runs over, the one named last changes fastest.
Arguments:
- queries: bfloat16 [131072, 1024], P('ctx', 'head'), may hold values from -240 to 240
- key_rows: bfloat16 [131072, 128], P(('ctx', 'head')), may hold values from -7 to 7
- value_rows: bfloat16 [131072, 128], P(('ctx', 'head')), may hold values from -6 to 6
- doc_ids: int32 [131072], replicated, may hold values from 0 to 63, never falling along the last dimension, each value on 1 to 8192 neighbouring positions
Outputs:
- attended: bfloat16 [131072, 1024], P('ctx', 'head')
Inputs may be any that keep to these rules, and one draw needn't show every extreme that they name: `doc_ids`: every document has between 1 and 8192 positions and one has exactly 8192; all 64 numbers occur.
All inputs are finite; a program needn't handle non-finite values.
Results may differ from a plain program's by a relative error of at most 0.0039.
Values may be sent and summed in bfloat16 or wider, within the bound.
No kernel may reach another device: no remote copies, remote signals or barrier semaphores. Data moves between devices by JAX's collectives and lax.ppermute only.
A program may use at most 64 MiB of HBM per device.

v0:
```python
import functools
import math

import jax
import jax.numpy as jnp
from jax import lax
from jax.experimental import pallas as pl
from jax.experimental.pallas import tpu as pltpu
from jax.sharding import PartitionSpec as P


PRIOR = 4
DOCS = 64
TQ = 1024
SUB = 512
SAFE = 256
NEAR = 3
HIGH = 1e30
LOW = 1e-18
NEG = -1e30
VMEM_BYTES = 24 << 20


def ctx_shift(block, distance):
    n = lax.axis_size("ctx")
    return lax.ppermute(block, "ctx", [(i, i + distance) for i in range(n - distance)])


def y_shift(block, distance):
    n = lax.axis_size("head")
    return lax.ppermute(block, "head", [(i, (i + 2 * distance) % n) for i in range(n)])


def core_swap(block):
    n = lax.axis_size("head")
    return lax.ppermute(block, "head", [(i, i ^ 1) for i in range(n)])


def score_halves(q, k):
    s = lax.dot_general(q, k, (((1,), (1,)), ((), ())), preferred_element_type=jnp.float32)
    return [s[:, j : j + 128] for j in range(0, s.shape[1], 128)]


def allowed(base, ds, qpos):
    out = []
    for j in range(2):
        kpos = base + j * 128 + lax.broadcasted_iota(jnp.int32, ds.shape, 1)
        out.append((kpos >= ds) & (kpos <= qpos))
    return out


def add_pieces(scale, rows, q_ref, ds_ref, l_ref, a_ref, lead, pieces, bases=None):
    for r in range(0, rows.size, SUB):
        at = pl.ds(pl.multiple_of(rows.start + r, SUB), SUB)
        q = q_ref[at, :]
        if bases is not None:
            ds = ds_ref[at, :]
            qpos = lead + rows.start + r + lax.broadcasted_iota(jnp.int32, ds.shape, 0)
        probs = []
        for n, (k, _) in enumerate(pieces):
            xs = [s * scale for s in score_halves(q, k)]
            if bases is not None:
                xs = [jnp.where(ok, x, NEG) for x, ok in zip(xs, allowed(bases[n], ds, qpos))]
            probs += [jnp.exp2(x) for x in xs]
        l_ref[at, :] += functools.reduce(jnp.add, probs)
        p = jnp.concatenate([t.astype(jnp.bfloat16) for t in probs], axis=1)
        values = jnp.concatenate([v for _, v in pieces], axis=0) if len(pieces) > 1 else pieces[0][1]
        a_ref[at, :] += jnp.dot(p, values, preferred_element_type=jnp.float32)


def safe_piece(scale, rows, q_ref, ds_ref, m_ref, l_ref, a_ref, lead, piece, base):
    k, v = piece
    ds = ds_ref[rows, :]
    qpos = lead + rows.start + lax.broadcasted_iota(jnp.int32, ds.shape, 0)
    oks = allowed(base, ds, qpos)
    ss = [jnp.where(ok, s, NEG) for s, ok in zip(score_halves(q_ref[rows, :], k), oks)]
    old = m_ref[rows, :]
    top = jnp.max(functools.reduce(jnp.maximum, ss), axis=1, keepdims=True)
    m = jnp.maximum(old, jnp.broadcast_to(top, old.shape))
    keep = jnp.exp2((old - m) * scale)
    probs = [jnp.where(ok, jnp.exp2((s - m) * scale), 0.0) for s, ok in zip(ss, oks)]
    m_ref[rows, :] = m
    l_ref[rows, :] = l_ref[rows, :] * keep + functools.reduce(jnp.add, probs)
    p = jnp.concatenate([t.astype(jnp.bfloat16) for t in probs], axis=1)
    a_ref[rows, :] = a_ref[rows, :] * keep + jnp.dot(p, v, preferred_element_type=jnp.float32)


def row_slice(tile, size):
    return pl.ds(pl.multiple_of(tile * size, size), size)


def split(ref, index):
    half = ref.shape[1] // 2
    return ref[index, :half, :], ref[index, half:, :]


def attend_kernel(scale, tok, count, groups, everything, first_step, meta, edges, q_ref, *refs):
    arrays = refs[:count]
    ds_ref = refs[count]
    if first_step:
        l_ref, a_ref = refs[count + 1 :]
    elif everything is None:
        l_in, a_in, l_ref, a_ref = refs[count + 1 :]
    else:
        l_in, a_in, out_ref, l_ref, a_ref, m_ref = refs[count + 1 :]
    rows_of = arrays[0].shape[1] // 2
    lead = PRIOR * tok
    per = edges.shape[0] // 2 // (tok // TQ)
    state = (q_ref, ds_ref, l_ref, a_ref, lead)

    @pl.loop(0, tok // TQ)
    def _(tile):
        rows = row_slice(tile, TQ)
        first, last = edges[2 * per * tile], edges[2 * per * (tile + 1) - 1]
        end = lead + (tile + 1) * TQ
        if first_step:
            l_ref[rows, :] = jnp.zeros((TQ, l_ref.shape[1]), jnp.float32)
            a_ref[rows, :] = jnp.zeros((TQ, a_ref.shape[1]), jnp.float32)
        else:
            l_ref[rows, :] = l_in[rows, :]
            a_ref[rows, :] = a_in[rows, :]

        for near, pieces, slots in groups:

            @pl.loop(0, pieces)
            def _(index, near=near, slots=slots):
                distance = near + index
                start = lead - distance * tok
                full = jnp.logical_and(distance > 0, start >= last)
                bases = [start + rows_of * meta[slot] for _, _, slot in slots]
                wanted = [jnp.logical_and(base + rows_of > first, base < end) for base in bases]
                every = functools.reduce(jnp.logical_and, wanted)

                def update(which, mask):
                    taken = [split(arrays[slots[n][0]], slots[n][1] + index) for n in which]
                    add_pieces(scale, rows, *state, taken, [bases[n] for n in which] if mask else None)

                @pl.when(full)
                def _():
                    update(range(len(slots)), False)

                if len(slots) > 1:

                    @pl.when(jnp.logical_and(jnp.logical_not(full), every))
                    def _():
                        update(range(len(slots)), True)

                    alone = jnp.logical_not(jnp.logical_or(full, every))
                else:
                    alone = jnp.logical_not(full)
                for n in range(len(slots)):

                    @pl.when(jnp.logical_and(wanted[n], alone))
                    def _(n=n):
                        update([n], True)

        if everything is not None:
            total = jnp.sum(l_ref[rows, :], axis=1, keepdims=True)
            good = jnp.logical_and(jnp.max(total) < HIGH, jnp.min(total) > LOW)

            @pl.when(jnp.logical_not(good))
            def _():
                @pl.loop(0, TQ // SAFE)
                def _(part):
                    some = row_slice(tile * (TQ // SAFE) + part, SAFE)
                    m_ref[some, :] = jnp.full((SAFE, m_ref.shape[1]), NEG, jnp.float32)
                    l_ref[some, :] = jnp.zeros((SAFE, l_ref.shape[1]), jnp.float32)
                    a_ref[some, :] = jnp.zeros((SAFE, a_ref.shape[1]), jnp.float32)
                    for near, pieces, slots in everything:
                        for array, offset, slot in slots:

                            @pl.loop(0, pieces)
                            def _(index, near=near, array=array, offset=offset, slot=slot):
                                base = lead - (near + index) * tok + rows_of * meta[slot]

                                @pl.when(jnp.logical_and(base + rows_of > first, base < end))
                                def _():
                                    piece = split(arrays[array], offset + index)
                                    safe_piece(scale, some, q_ref, ds_ref, m_ref, l_ref, a_ref, lead, piece, base)

            total = jnp.sum(l_ref[rows, :], axis=1, keepdims=True)
            out_ref[rows, :] = (a_ref[rows, :] / total).astype(out_ref.dtype)


def pack_kernel(k_ref, v_ref, out_ref, sems):
    rows = k_ref.shape[0]
    copies = [
        pltpu.make_async_copy(k_ref, out_ref.at[:rows, :], sems.at[0]),
        pltpu.make_async_copy(v_ref, out_ref.at[rows:, :], sems.at[1]),
    ]
    for copy in copies:
        copy.start()
    for copy in copies:
        copy.wait()


SMEM = pl.BlockSpec(memory_space=pltpu.SMEM)
VMEM = pl.BlockSpec(memory_space=pltpu.VMEM)
ANY = pl.BlockSpec(memory_space=pl.ANY)


def body(queries, key_rows, value_rows, doc_ids):
    tok, hd = queries.shape
    rows_of = key_rows.shape[0]
    n_y = lax.axis_size("head") // 2
    scale = math.log2(math.e) / math.sqrt(hd)
    ctx = lax.axis_index("ctx")
    head = lax.axis_index("head")
    y, core = head // 2, head % 2

    own = pl.pallas_call(
        pack_kernel,
        out_shape=jax.ShapeDtypeStruct((2 * rows_of, hd), key_rows.dtype),
        in_specs=[ANY] * 2,
        out_specs=VMEM,
        scratch_shapes=[pltpu.SemaphoreType.DMA((2,))],
        compiler_params=pltpu.CompilerParams(vmem_limit_bytes=1 << 20),
        name="pack",
    )(key_rows, value_rows)
    z1 = ctx_shift(own, 1)
    z2 = ctx_shift(own, 2)

    window = jnp.concatenate([jnp.full((PRIOR * tok,), -1, jnp.int32), doc_ids])
    window = lax.optimization_barrier(lax.dynamic_slice_in_dim(window, ctx * tok, (PRIOR + 1) * tok, 0))
    own_ids = window[PRIOR * tok :]
    docs = jnp.arange(DOCS, dtype=jnp.int32)
    counts = jnp.sum((window[None, :] < docs[:, None]).astype(jnp.int32), axis=1)
    ds = jnp.sum(jnp.where(own_ids[:, None] == docs[None, :], counts[None, :], 0), axis=1)
    edges = jnp.stack([ds[:: 2 * rows_of], ds[2 * rows_of - 1 :: 2 * rows_of]], axis=1).reshape(-1)
    ds = jnp.broadcast_to(ds[:, None], (tok, 128))
    up, down, far = (y + n_y - 1) % n_y, (y + 1) % n_y, (y + 2) % n_y
    meta = jnp.stack(
        [head, core, 2 * y + 1 - core, 2 * up + core, 2 * down + core, 2 * up + 1 - core, 2 * down + 1 - core]
        + [2 * far + core, 2 * far + 1 - core]
    ).astype(jnp.int32)
    z1, z2, ds, meta, edges = lax.optimization_barrier((z1, z2, ds, meta, edges))

    near = jnp.stack([z1, z2])
    g1 = jnp.stack([own, z1, z2])
    g2 = ctx_shift(near, 2)
    up1 = y_shift(g1, 1)
    down1 = y_shift(g1, -1)

    def step(arrays, groups, state, everything=None):
        shapes = [jax.ShapeDtypeStruct((tok, 128), jnp.float32), jax.ShapeDtypeStruct((tok, hd), jnp.float32)]
        scratch = []
        if everything is not None:
            scratch = [pltpu.VMEM(s.shape, s.dtype) for s in shapes + shapes[:1]]
            shapes = [jax.ShapeDtypeStruct((tok, hd), queries.dtype)]
        keys = sum(pieces * len(slots) * rows_of for _, pieces, slots in groups)
        return pl.pallas_call(
            functools.partial(attend_kernel, scale, tok, len(arrays), groups, everything, not state),
            out_shape=shapes,
            in_specs=[SMEM, SMEM] + [VMEM] * (len(arrays) + 2 + len(state)),
            out_specs=[VMEM] * len(shapes),
            scratch_shapes=scratch,
            cost_estimate=pl.CostEstimate(
                flops=4 * tok * keys * hd, bytes_accessed=4 << 20, transcendentals=tok * keys
            ),
            compiler_params=pltpu.CompilerParams(vmem_limit_bytes=VMEM_BYTES),
        )(meta, edges, queries, *arrays, ds, *state)

    count = PRIOR + 1
    far_count = count - NEAR
    state = step([g1], [(0, NEAR, [(0, 0, 0)])], [])
    up1, g2, state = lax.optimization_barrier((up1, g2, state))
    down2 = y_shift(g2, -1)
    up2 = y_shift(g2, 1)
    far1 = y_shift(up1, 1)
    state = step([up1, down1], [(0, NEAR, [(0, 0, 3), (1, 0, 4)])], state)
    down2, state = lax.optimization_barrier((down2, state))
    far2 = y_shift(down2, -1)
    state = step([g2, up2, down2], [(NEAR, far_count, [(0, 0, 0), (1, 0, 3), (2, 0, 4)])], state)
    far1, far2, state = lax.optimization_barrier((far1, far2, state))
    held = jnp.concatenate([g1, g2, up1, up2, down1, down2, far1, far2], axis=0)
    crossed = core_swap(held)
    state = step([held], [(0, count, [(0, 3 * count, 7)])], state)
    groups = [(0, count, [(0, n * count, slot) for n, slot in enumerate((2, 5, 6, 8))])]
    earlier = [(0, count, [(1, n * count, slot) for n, slot in enumerate((0, 3, 4, 7))])]
    return step([crossed, held], groups, state, everything=groups + earlier)[0]


def solution(mesh):
    in_specs = (P("ctx", "head"), P(("ctx", "head"), None), P(("ctx", "head"), None), P())
    return jax.shard_map(body, mesh=mesh, in_specs=in_specs, out_specs=P("ctx", "head"), check_vma=False)
```

profile of v0, /device:TPU:30, one launch (start us, length us, event | category | flops | bytes accessed | tf_op | source)
XLA Modules:
  0.0 204.7 jit_solution(15207394547211011804)
XLA Ops:
  0.0 0.8 copy-done.1
  0.8 0.8 copy-done.2
  1.9 3.8 %collective-permute-start = (bf16[512,128]{1,0:T(8,128)(2,1)S(1)}, bf16[512,128]{1,0:T(8,128)(2,1)S(1)}, u32[]{:S(2)}, u32[]{:S(2)}) collective-permute-start(bf16[512,128]{1,0:T(8,128)(2,1)S(1)} %pack.1), channel_id=1, source_target_pairs={{0,8},{8,16},{16,24},{24,32},{32,40},{40,48},{48,56},{56,64},{64,7... | collective-permute-start | bytes 393224 | tf_op jit(solution)/shard_map/ppermute | solution.py:26
  5.7 5.2 %collective-permute-start.1 = (bf16[512,128]{1,0:T(8,128)(2,1)S(1)}, bf16[512,128]{1,0:T(8,128)(2,1)S(1)}, u32[]{:S(2)}, u32[]{:S(2)}) collective-permute-start(bf16[512,128]{1,0:T(8,128)(2,1)S(1)} %pack.1), channel_id=1, source_target_pairs={{0,16},{8,24},{16,32},{24,40},{32,48},{40,56},{48,64},{56,72},{64,... | collective-permute-start | bytes 393224 | tf_op jit(solution)/shard_map/ppermute | solution.py:26
  10.9 0.8 pad_dynamic-slice_fusion
  11.7 0.4 convert_reduce_fusion
  12.8 5.6 %collective-permute-done = bf16[512,128]{1,0:T(8,128)(2,1)S(1)} collective-permute-done((bf16[512,128]{1,0:T(8,128)(2,1)S(1)}, bf16[512,128]{1,0:T(8,128)(2,1)S(1)}, u32[]{:S(2)}, u32[]{:S(2)}) %collective-permute-start) | collective-permute-done | bytes 131104 | tf_op jit(solution)/shard_map/ppermute | solution.py:26
  18.3 4.5 %collective-permute-done.1 = bf16[512,128]{1,0:T(8,128)(2,1)S(1)} collective-permute-done((bf16[512,128]{1,0:T(8,128)(2,1)S(1)}, bf16[512,128]{1,0:T(8,128)(2,1)S(1)}, u32[]{:S(2)}, u32[]{:S(2)}) %collective-permute-start.1) | collective-permute-done | bytes 131104 | tf_op jit(solution)/shard_map/ppermute | solution.py:26
  22.8 0.3 broadcast_in_dim.16.refs_1_.refs_2_.refs_3_
  23.2 2.1 %collective-permute-start.2 = (bf16[3,512,128]{2,1,0:T(8,128)(2,1)S(1)}, bf16[3,512,128]{2,1,0:T(8,128)(2,1)S(1)}, u32[]{:S(2)}, u32[]{:S(2)}) collective-permute-start(bf16[3,512,128]{2,1,0:T(8,128)(2,1)S(1)} %pad_maximum_fusion.refs_0_), channel_id=1, source_target_pairs={{0,2},{1,3},{2,4},{3,5},{4,6},{5,7},{6,0},{7,1},{8,10},{9,11},{10,... | collective-permute-start | bytes 1179656 | tf_op jit(solution)/shard_map/ppermute | solution.py:31
  25.3 3.7 %collective-permute-start.5 = (bf16[3,512,128]{2,1,0:T(8,128)(2,1)S(1)}, bf16[3,512,128]{2,1,0:T(8,128)(2,1)S(1)}, u32[]{:S(2)}, u32[]{:S(2)}) collective-permute-start(bf16[3,512,128]{2,1,0:T(8,128)(2,1)S(1)} %pad_maximum_fusion.refs_0_), channel_id=1, source_target_pairs={{0,6},{1,7},{2,0},{3,1},{4,2},{5,3},{6,4},{7,5},{8,14},{9,15},{10,... | collective-permute-start | bytes 1179656 | tf_op jit(solution)/shard_map/ppermute | solution.py:31
  29.1 1.9 collective-permute-start.3
  31.1 3.5 %shard_map.46 = (f32[2048,128]{1,0:T(8,128)S(1)}, f32[2048,128]{1,0:T(8,128)S(1)}) custom-call(s32[9]{0:T(128)S(1)} %stack.65.meta, s32[8]{0:T(128)S(1)} %reshape.7.edges, bf16[2048,128]{1,0:T(8,128)(2,1)S(1)} %copy-done, bf16[3,512,128]{2,1,0:T(8,128)(2,1)S(1)} %pad_maximum_fusion.refs_0_, s32[2048,128]{1,0:T(8,128)S(1)} %broadcast_in_dim.16.refs_1_.refs_2_.refs_3_), custom_call_target="tpu_custom_call" | custom-call | flops 805306368 | bytes 4194304 | tf_op jit(solution)/shard_map/pallas_call | solution.py:251
  34.6 11.0 %collective-permute-done.3.refs_0_ = bf16[2,512,128]{2,1,0:T(8,128)(2,1)S(1)} collective-permute-done((bf16[2,512,128]{2,1,0:T(8,128)(2,1)S(1)}, bf16[2,512,128]{2,1,0:T(8,128)(2,1)S(1)}, u32[]{:S(2)}, u32[]{:S(2)}) %collective-permute-start.3) | collective-permute-done | bytes 262176 | tf_op jit(solution)/shard_map/ppermute | solution.py:26
  45.6 3.4 %collective-permute-start.4 = (bf16[2,512,128]{2,1,0:T(8,128)(2,1)S(1)}, bf16[2,512,128]{2,1,0:T(8,128)(2,1)S(1)}, u32[]{:S(2)}, u32[]{:S(2)}) collective-permute-start(bf16[2,512,128]{2,1,0:T(8,128)(2,1)S(1)} %collective-permute-done.3.refs_0_), channel_id=1, source_target_pairs={{0,2},{1,3},{2,4},{3,5},{4,6},{5,7},{6,0},{7,1},{8,10},{9,11},{10,... | collective-permute-start | bytes 786440 | tf_op jit(solution)/shard_map/ppermute | solution.py:31
  49.0 2.4 %collective-permute-start.6 = (bf16[2,512,128]{2,1,0:T(8,128)(2,1)S(1)}, bf16[2,512,128]{2,1,0:T(8,128)(2,1)S(1)}, u32[]{:S(2)}, u32[]{:S(2)}) collective-permute-start(bf16[2,512,128]{2,1,0:T(8,128)(2,1)S(1)} %collective-permute-done.3.refs_0_), channel_id=1, source_target_pairs={{0,6},{1,7},{2,0},{3,1},{4,2},{5,3},{6,4},{7,5},{8,14},{9,15},{10,... | collective-permute-start | bytes 786440 | tf_op jit(solution)/shard_map/ppermute | solution.py:31
  51.4 4.6 %collective-permute-start.7 = (bf16[3,512,128]{2,1,0:T(8,128)(2,1)S(1)}, bf16[3,512,128]{2,1,0:T(8,128)(2,1)S(1)}, u32[]{:S(2)}, u32[]{:S(2)}) collective-permute-start(bf16[3,512,128]{2,1,0:T(8,128)(2,1)S(1)} %collective-permute-done.2.refs_0_), channel_id=1, source_target_pairs={{0,2},{1,3},{2,4},{3,5},{4,6},{5,7},{6,0},{7,1},{8,10},{9,11},{10,... | collective-permute-start | bytes 1179656 | tf_op jit(solution)/shard_map/ppermute | solution.py:31
  56.2 5.9 %shard_map.47 = (f32[2048,128]{1,0:T(8,128)S(1)}, f32[2048,128]{1,0:T(8,128)S(1)}) custom-call(s32[9]{0:T(128)S(1)} %stack.65.meta, s32[8]{0:T(128)S(1)} %reshape.7.edges, bf16[2048,128]{1,0:T(8,128)(2,1)S(1)} %copy-done, bf16[3,512,128]{2,1,0:T(8,128)(2,1)S(1)} %collective-permute-done.2.refs_0_, bf16[3,512,128]{2,1,0:T(8,128)(2,1)S(1)} %collective-permute-done.5.refs_1_, ...), custom_call_target="tpu_custom_call" | custom-call | flops 1610612736 | bytes 4194304 | tf_op jit(solution)/shard_map/pallas_call | solution.py:251
  62.1 1.9 collective-permute-start.8
  64.2 3.1 %shard_map.48 = (f32[2048,128]{1,0:T(8,128)S(1)}, f32[2048,128]{1,0:T(8,128)S(1)}) custom-call(s32[9]{0:T(128)S(1)} %stack.65.meta, s32[8]{0:T(128)S(1)} %reshape.7.edges, bf16[2048,128]{1,0:T(8,128)(2,1)S(1)} %copy-done, bf16[2,512,128]{2,1,0:T(8,128)(2,1)S(1)} %collective-permute-done.3.refs_0_, bf16[2,512,128]{2,1,0:T(8,128)(2,1)S(1)} %collective-permute-done.4.refs_1_, ...), custom_call_target="tpu_custom_call" | custom-call | flops 1610612736 | bytes 4194304 | tf_op jit(solution)/shard_map/pallas_call | solution.py:251
  67.3 4.2 %collective-permute-done.8 = bf16[2,512,128]{2,1,0:T(8,128)(2,1)S(1)} collective-permute-done((bf16[2,512,128]{2,1,0:T(8,128)(2,1)S(1)}, bf16[2,512,128]{2,1,0:T(8,128)(2,1)S(1)}, u32[]{:S(2)}, u32[]{:S(2)}) %collective-permute-start.8) | collective-permute-done | bytes 262176 | tf_op jit(solution)/shard_map/ppermute | solution.py:31
  71.7 2.1 %collective-permute-start.9 = (bf16[20,512,128]{2,1,0:T(8,128)(2,1)S(1)}, bf16[20,512,128]{2,1,0:T(8,128)(2,1)S(1)}, u32[]{:S(2)}, u32[]{:S(2)}) collective-permute-start(bf16[20,512,128]{2,1,0:T(8,128)(2,1)S(1)} %constant_dynamic-update-slice_fusion.refs_0_.refs_1_), channel_id=1, source_target_pairs={{0,1},{1,0},{2,3},{3,2},{4,5},{5,4},{6,7},{7,6},{8,9},{9,8},{10,11... | collective-permute-start | bytes 7864328 | tf_op jit(solution)/shard_map/ppermute | solution.py:36
  73.8 5.3 %shard_map.49 = (f32[2048,128]{1,0:T(8,128)S(1)}, f32[2048,128]{1,0:T(8,128)S(1)}) custom-call(s32[9]{0:T(128)S(1)} %stack.65.meta, s32[8]{0:T(128)S(1)} %reshape.7.edges, bf16[2048,128]{1,0:T(8,128)(2,1)S(1)} %copy-done, bf16[20,512,128]{2,1,0:T(8,128)(2,1)S(1)} %constant_dynamic-update-slice_fusion.refs_0_.refs_1_, ...), custom_call_target="tpu_custom_call" | custom-call | flops 1342177280 | bytes 4194304 | tf_op jit(solution)/shard_map/pallas_call | solution.py:251
  79.0 125.6 %shard_map.50 = bf16[2048,128]{1,0:T(8,128)(2,1)} custom-call(s32[9]{0:T(128)S(1)} %stack.65.meta, s32[8]{0:T(128)S(1)} %reshape.7.edges, bf16[2048,128]{1,0:T(8,128)(2,1)S(1)} %copy-done, bf16[20,512,128]{2,1,0:T(8,128)(2,1)S(1)} %collective-permute-done.9.refs_0_, bf16[20,512,128]{2,1,0:T(8,128)(2,1)S(1)} %constant_dynamic-update-slice_fusion.refs_0_.refs_1_, ...), custom_call_target="tpu_custom_call" | custom-call | flops 5368709120 | bytes 4194304 | tf_op jit(solution)/shard_map/pallas_call | solution.py:251
  (31 shorter events, 1.2 us)
Async XLA Ops:
  0.0 0.8 copy-start.1
  0.8 0.8 copy-start.2
  1.7 29.4 %copy-start = (bf16[2048,128]{1,0:T(8,128)(2,1)S(1)}, bf16[2048,128]{1,0:T(8,128)(2,1)}, u32[]{:S(2)}) copy-start(bf16[2048,128]{1,0:T(8,128)(2,1)} %q_ref.9) | copy-start | bytes 1572868
  1.9 16.5 %collective-permute-start = (bf16[512,128]{1,0:T(8,128)(2,1)S(1)}, bf16[512,128]{1,0:T(8,128)(2,1)S(1)}, u32[]{:S(2)}, u32[]{:S(2)}) collective-permute-start(bf16[512,128]{1,0:T(8,128)(2,1)S(1)} %pack.1), channel_id=1, source_target_pairs={{0,8},{8,16},{16,24},{24,32},{32,40},{40,48},{48,56},{56,64},{64,7... | collective-permute-start | bytes 393224 | tf_op jit(solution)/shard_map/ppermute | solution.py:26
  5.7 17.1 %collective-permute-start.1 = (bf16[512,128]{1,0:T(8,128)(2,1)S(1)}, bf16[512,128]{1,0:T(8,128)(2,1)S(1)}, u32[]{:S(2)}, u32[]{:S(2)}) collective-permute-start(bf16[512,128]{1,0:T(8,128)(2,1)S(1)} %pack.1), channel_id=1, source_target_pairs={{0,16},{8,24},{16,32},{24,40},{32,48},{40,56},{48,64},{56,72},{64,... | collective-permute-start | bytes 393224 | tf_op jit(solution)/shard_map/ppermute | solution.py:26
  23.2 22.4 %collective-permute-start.2 = (bf16[3,512,128]{2,1,0:T(8,128)(2,1)S(1)}, bf16[3,512,128]{2,1,0:T(8,128)(2,1)S(1)}, u32[]{:S(2)}, u32[]{:S(2)}) collective-permute-start(bf16[3,512,128]{2,1,0:T(8,128)(2,1)S(1)} %pad_maximum_fusion.refs_0_), channel_id=1, source_target_pairs={{0,2},{1,3},{2,4},{3,5},{4,6},{5,7},{6,0},{7,1},{8,10},{9,11},{10,... | collective-permute-start | bytes 1179656 | tf_op jit(solution)/shard_map/ppermute | solution.py:31
  25.3 30.8 %collective-permute-start.5 = (bf16[3,512,128]{2,1,0:T(8,128)(2,1)S(1)}, bf16[3,512,128]{2,1,0:T(8,128)(2,1)S(1)}, u32[]{:S(2)}, u32[]{:S(2)}) collective-permute-start(bf16[3,512,128]{2,1,0:T(8,128)(2,1)S(1)} %pad_maximum_fusion.refs_0_), channel_id=1, source_target_pairs={{0,6},{1,7},{2,0},{3,1},{4,2},{5,3},{6,4},{7,5},{8,14},{9,15},{10,... | collective-permute-start | bytes 1179656 | tf_op jit(solution)/shard_map/ppermute | solution.py:31
  29.1 16.5 %collective-permute-start.3 = (bf16[2,512,128]{2,1,0:T(8,128)(2,1)S(1)}, bf16[2,512,128]{2,1,0:T(8,128)(2,1)S(1)}, u32[]{:S(2)}, u32[]{:S(2)}) collective-permute-start(bf16[2,512,128]{2,1,0:T(8,128)(2,1)S(1)} %pad_maximum_fusion.1), channel_id=1, source_target_pairs={{0,16},{8,24},{16,32},{24,40},{32,48},{40,56},{48,64},{56,72},{64,... | collective-permute-start | bytes 786440 | tf_op jit(solution)/shard_map/ppermute | solution.py:26
  45.6 18.4 %collective-permute-start.4 = (bf16[2,512,128]{2,1,0:T(8,128)(2,1)S(1)}, bf16[2,512,128]{2,1,0:T(8,128)(2,1)S(1)}, u32[]{:S(2)}, u32[]{:S(2)}) collective-permute-start(bf16[2,512,128]{2,1,0:T(8,128)(2,1)S(1)} %collective-permute-done.3.refs_0_), channel_id=1, source_target_pairs={{0,2},{1,3},{2,4},{3,5},{4,6},{5,7},{6,0},{7,1},{8,10},{9,11},{10,... | collective-permute-start | bytes 786440 | tf_op jit(solution)/shard_map/ppermute | solution.py:31
  49.0 13.1 %collective-permute-start.6 = (bf16[2,512,128]{2,1,0:T(8,128)(2,1)S(1)}, bf16[2,512,128]{2,1,0:T(8,128)(2,1)S(1)}, u32[]{:S(2)}, u32[]{:S(2)}) collective-permute-start(bf16[2,512,128]{2,1,0:T(8,128)(2,1)S(1)} %collective-permute-done.3.refs_0_), channel_id=1, source_target_pairs={{0,6},{1,7},{2,0},{3,1},{4,2},{5,3},{6,4},{7,5},{8,14},{9,15},{10,... | collective-permute-start | bytes 786440 | tf_op jit(solution)/shard_map/ppermute | solution.py:31
  51.4 15.9 %collective-permute-start.7 = (bf16[3,512,128]{2,1,0:T(8,128)(2,1)S(1)}, bf16[3,512,128]{2,1,0:T(8,128)(2,1)S(1)}, u32[]{:S(2)}, u32[]{:S(2)}) collective-permute-start(bf16[3,512,128]{2,1,0:T(8,128)(2,1)S(1)} %collective-permute-done.2.refs_0_), channel_id=1, source_target_pairs={{0,2},{1,3},{2,4},{3,5},{4,6},{5,7},{6,0},{7,1},{8,10},{9,11},{10,... | collective-permute-start | bytes 1179656 | tf_op jit(solution)/shard_map/ppermute | solution.py:31
  62.1 9.5 %collective-permute-start.8 = (bf16[2,512,128]{2,1,0:T(8,128)(2,1)S(1)}, bf16[2,512,128]{2,1,0:T(8,128)(2,1)S(1)}, u32[]{:S(2)}, u32[]{:S(2)}) collective-permute-start(bf16[2,512,128]{2,1,0:T(8,128)(2,1)S(1)} %collective-permute-done.6.refs_2_), channel_id=1, source_target_pairs={{0,6},{1,7},{2,0},{3,1},{4,2},{5,3},{6,4},{7,5},{8,14},{9,15},{10,... | collective-permute-start | bytes 786440 | tf_op jit(solution)/shard_map/ppermute | solution.py:31
  71.7 7.4 %collective-permute-start.9 = (bf16[20,512,128]{2,1,0:T(8,128)(2,1)S(1)}, bf16[20,512,128]{2,1,0:T(8,128)(2,1)S(1)}, u32[]{:S(2)}, u32[]{:S(2)}) collective-permute-start(bf16[20,512,128]{2,1,0:T(8,128)(2,1)S(1)} %constant_dynamic-update-slice_fusion.refs_0_.refs_1_), channel_id=1, source_target_pairs={{0,1},{1,0},{2,3},{3,2},{4,5},{5,4},{6,7},{7,6},{8,9},{9,8},{10,11... | collective-permute-start | bytes 7864328 | tf_op jit(solution)/shard_map/ppermute | solution.py:36
where the time goes:
time: 205 us
  Pallas kernels  144 us (70%)
  starting transfers between devices  31.2 us (15%)
  waiting for transfers between devices  25.2 us (12%)
  local copies, waits for them, and re-layouts  3.6 us (2%)
    pallas_call x5, Pallas kernels, step(): pl.pallas_call(functools.partial(attend_kernel, scale, tok, len(arrays),...  143 us
    ppermute x3, waiting for transfers between devices, ctx_shift(): lax.ppermute(block, 'ctx', [(i, i + distance) for i in range(n - distance)])  21 us
    ppermute x6, starting transfers between devices, y_shift(): lax.ppermute(block, 'head', [(i, (i + 2 * distance) % n) for i in range(n)])  18.2 us
    ppermute x3, starting transfers between devices, ctx_shift(): lax.ppermute(block, 'ctx', [(i, i + distance) for i in range(n - distance)])  10.9 us
    ppermute x6, waiting for transfers between devices, y_shift(): lax.ppermute(block, 'head', [(i, (i + 2 * distance) % n) for i in range(n)])  4.24 us
  transfers between devices with their start and end apart: 10, of which 4 were waited for; matrix products, arithmetic and copies ran while one was open for 1% of the time, Pallas kernels for 9%

commit v1 on v0

--- a/solution.py
+++ b/solution.py
@@ -126,8 +126,9 @@
             def _(index, near=near, slots=slots):
                 distance = near + index
                 start = lead - distance * tok
-                full = jnp.logical_and(distance > 0, start >= last)
-                bases = [start + rows_of * meta[slot] for _, _, slot in slots]
+                deepest = start - max(more for _, _, _, more in slots) * tok
+                full = jnp.logical_and(distance > 0, deepest >= last)
+                bases = [start - more * tok + rows_of * meta[slot] for _, _, slot, more in slots]
                 wanted = [jnp.logical_and(base + rows_of > first, base < end) for base in bases]
                 every = functools.reduce(jnp.logical_and, wanted)
 
@@ -155,8 +156,12 @@
                         update([n], True)
 
         if everything is not None:
+            def finish(total):
+                out_ref[rows, :] = (a_ref[rows, :] / total).astype(out_ref.dtype)
+
             total = jnp.sum(l_ref[rows, :], axis=1, keepdims=True)
             good = jnp.logical_and(jnp.max(total) < HIGH, jnp.min(total) > LOW)
+            finish(total)
 
             @pl.when(jnp.logical_not(good))
             def _():
@@ -167,10 +172,10 @@
                     l_ref[some, :] = jnp.zeros((SAFE, l_ref.shape[1]), jnp.float32)
                     a_ref[some, :] = jnp.zeros((SAFE, a_ref.shape[1]), jnp.float32)
                     for near, pieces, slots in everything:
-                        for array, offset, slot in slots:
+                        for array, offset, slot, more in slots:
 
                             @pl.loop(0, pieces)
-                            def _(index, near=near, array=array, offset=offset, slot=slot):
+                            def _(index, near=near + more, array=array, offset=offset, slot=slot):
                                 base = lead - (near + index) * tok + rows_of * meta[slot]
 
                                 @pl.when(jnp.logical_and(base + rows_of > first, base < end))
@@ -178,8 +183,7 @@
                                     piece = split(arrays[array], offset + index)
                                     safe_piece(scale, some, q_ref, ds_ref, m_ref, l_ref, a_ref, lead, piece, base)
 
-            total = jnp.sum(l_ref[rows, :], axis=1, keepdims=True)
-            out_ref[rows, :] = (a_ref[rows, :] / total).astype(out_ref.dtype)
+                finish(jnp.sum(l_ref[rows, :], axis=1, keepdims=True))
 
 
 def pack_kernel(k_ref, v_ref, out_ref, sems):
@@ -262,21 +266,24 @@
 
     count = PRIOR + 1
     far_count = count - NEAR
-    state = step([g1], [(0, NEAR, [(0, 0, 0)])], [])
+    state = step([g1], [(0, 1, [(0, 0, 0, 0)]), (1, 1, [(0, 1, 0, 0), (0, 2, 0, 1)])], [])
     up1, g2, state = lax.optimization_barrier((up1, g2, state))
     down2 = y_shift(g2, -1)
     up2 = y_shift(g2, 1)
     far1 = y_shift(up1, 1)
-    state = step([up1, down1], [(0, NEAR, [(0, 0, 3), (1, 0, 4)])], state)
+    both = [(0, 1, 3, 0), (1, 1, 4, 0), (0, 2, 3, 1), (1, 2, 4, 1)]
+    state = step([up1, down1], [(0, 1, [(0, 0, 3, 0), (1, 0, 4, 0)]), (1, 1, both)], state)
     down2, state = lax.optimization_barrier((down2, state))
     far2 = y_shift(down2, -1)
-    state = step([g2, up2, down2], [(NEAR, far_count, [(0, 0, 0), (1, 0, 3), (2, 0, 4)])], state)
+    state = step([g2, up2, down2], [(NEAR, far_count, [(0, 0, 0, 0), (1, 0, 3, 0), (2, 0, 4, 0)])], state)
     far1, far2, state = lax.optimization_barrier((far1, far2, state))
     held = jnp.concatenate([g1, g2, up1, up2, down1, down2, far1, far2], axis=0)
     crossed = core_swap(held)
-    state = step([held], [(0, count, [(0, 3 * count, 7)])], state)
-    groups = [(0, count, [(0, n * count, slot) for n, slot in enumerate((2, 5, 6, 8))])]
-    earlier = [(0, count, [(1, n * count, slot) for n, slot in enumerate((0, 3, 4, 7))])]
+    at = 3 * count
+    pairs = [(d, 1, [(0, at + d, 7, 0), (0, at + d + 1, 7, 1)]) for d in (1, 3)]
+    state = step([held], [(0, 1, [(0, at, 7, 0)])] + pairs, state)
+    groups = [(0, count, [(0, n * count, slot, 0) for n, slot in enumerate((2, 5, 6, 8))])]
+    earlier = [(0, count, [(1, n * count, slot, 0) for n, slot in enumerate((0, 3, 4, 7))])]
     return step([crossed, held], groups, state, everything=groups + earlier)[0]
 
 

time: 205 us -> 204 us (level)
  transfers between devices with their start and end apart: 10 -> 10, of which waited for: 4 -> 5; matrix products, arithmetic and copies ran while one was open for 1% -> 1% of each run, Pallas kernels for 9% -> 8%
where the time goes in v1:
time: 204 us
  Pallas kernels  142 us (70%)
  starting transfers between devices  31.2 us (15%)
  waiting for transfers between devices  25.8 us (13%)
  local copies, waits for them, and re-layouts  3.6 us (2%)
    pallas_call x5, Pallas kernels, step(): pl.pallas_call(functools.partial(attend_kernel, scale, tok, len(arrays),...  142 us
    ppermute x3, waiting for transfers between devices, ctx_shift(): lax.ppermute(block, 'ctx', [(i, i + distance) for i in range(n - distance)])  21.6 us
    ppermute x6, starting transfers between devices, y_shift(): lax.ppermute(block, 'head', [(i, (i + 2 * distance) % n) for i in range(n)])  18.4 us
    ppermute x3, starting transfers between devices, ctx_shift(): lax.ppermute(block, 'ctx', [(i, i + distance) for i in range(n - distance)])  10.9 us
  transfers between devices with their start and end apart: 10, of which 5 were waited for; matrix products, arithmetic and copies ran while one was open for 1% of the time, Pallas kernels for 8%

profile of v1, /device:TPU:30, one launch (start us, length us, event | category | flops | bytes accessed | tf_op | source)
XLA Modules:
  0.0 203.9 jit_solution(1716948640789230021)
XLA Ops:
  0.0 0.8 copy-done.1
  0.8 0.8 copy-done.2
  1.9 3.8 %collective-permute-start = (bf16[512,128]{1,0:T(8,128)(2,1)S(1)}, bf16[512,128]{1,0:T(8,128)(2,1)S(1)}, u32[]{:S(2)}, u32[]{:S(2)}) collective-permute-start(bf16[512,128]{1,0:T(8,128)(2,1)S(1)} %pack.1), channel_id=1, source_target_pairs={{0,8},{8,16},{16,24},{24,32},{32,40},{40,48},{48,56},{56,64},{64,7... | collective-permute-start | bytes 393224 | tf_op jit(solution)/shard_map/ppermute | solution.py:26
  5.7 5.2 %collective-permute-start.1 = (bf16[512,128]{1,0:T(8,128)(2,1)S(1)}, bf16[512,128]{1,0:T(8,128)(2,1)S(1)}, u32[]{:S(2)}, u32[]{:S(2)}) collective-permute-start(bf16[512,128]{1,0:T(8,128)(2,1)S(1)} %pack.1), channel_id=1, source_target_pairs={{0,16},{8,24},{16,32},{24,40},{32,48},{40,56},{48,64},{56,72},{64,... | collective-permute-start | bytes 393224 | tf_op jit(solution)/shard_map/ppermute | solution.py:26
  10.9 0.8 pad_dynamic-slice_fusion
  11.7 0.4 convert_reduce_fusion
  12.8 5.6 %collective-permute-done = bf16[512,128]{1,0:T(8,128)(2,1)S(1)} collective-permute-done((bf16[512,128]{1,0:T(8,128)(2,1)S(1)}, bf16[512,128]{1,0:T(8,128)(2,1)S(1)}, u32[]{:S(2)}, u32[]{:S(2)}) %collective-permute-start) | collective-permute-done | bytes 131104 | tf_op jit(solution)/shard_map/ppermute | solution.py:26
  18.3 4.5 %collective-permute-done.1 = bf16[512,128]{1,0:T(8,128)(2,1)S(1)} collective-permute-done((bf16[512,128]{1,0:T(8,128)(2,1)S(1)}, bf16[512,128]{1,0:T(8,128)(2,1)S(1)}, u32[]{:S(2)}, u32[]{:S(2)}) %collective-permute-start.1) | collective-permute-done | bytes 131104 | tf_op jit(solution)/shard_map/ppermute | solution.py:26
  22.8 0.3 broadcast_in_dim.16.refs_1_.refs_2_.refs_3_
  23.2 2.1 %collective-permute-start.2 = (bf16[3,512,128]{2,1,0:T(8,128)(2,1)S(1)}, bf16[3,512,128]{2,1,0:T(8,128)(2,1)S(1)}, u32[]{:S(2)}, u32[]{:S(2)}) collective-permute-start(bf16[3,512,128]{2,1,0:T(8,128)(2,1)S(1)} %pad_maximum_fusion.refs_0_), channel_id=1, source_target_pairs={{0,2},{1,3},{2,4},{3,5},{4,6},{5,7},{6,0},{7,1},{8,10},{9,11},{10,... | collective-permute-start | bytes 1179656 | tf_op jit(solution)/shard_map/ppermute | solution.py:31
  25.3 3.7 %collective-permute-start.5 = (bf16[3,512,128]{2,1,0:T(8,128)(2,1)S(1)}, bf16[3,512,128]{2,1,0:T(8,128)(2,1)S(1)}, u32[]{:S(2)}, u32[]{:S(2)}) collective-permute-start(bf16[3,512,128]{2,1,0:T(8,128)(2,1)S(1)} %pad_maximum_fusion.refs_0_), channel_id=1, source_target_pairs={{0,6},{1,7},{2,0},{3,1},{4,2},{5,3},{6,4},{7,5},{8,14},{9,15},{10,... | collective-permute-start | bytes 1179656 | tf_op jit(solution)/shard_map/ppermute | solution.py:31
  29.1 1.9 collective-permute-start.3
  31.1 2.9 %shard_map.46 = (f32[2048,128]{1,0:T(8,128)S(1)}, f32[2048,128]{1,0:T(8,128)S(1)}) custom-call(s32[9]{0:T(128)S(1)} %stack.65.meta, s32[8]{0:T(128)S(1)} %reshape.7.edges, bf16[2048,128]{1,0:T(8,128)(2,1)S(1)} %copy-done, bf16[3,512,128]{2,1,0:T(8,128)(2,1)S(1)} %pad_maximum_fusion.refs_0_, s32[2048,128]{1,0:T(8,128)S(1)} %broadcast_in_dim.16.refs_1_.refs_2_.refs_3_), custom_call_target="tpu_custom_call" | custom-call | flops 805306368 | bytes 4194304 | tf_op jit(solution)/shard_map/pallas_call | solution.py:255
  34.0 11.5 %collective-permute-done.3.refs_0_ = bf16[2,512,128]{2,1,0:T(8,128)(2,1)S(1)} collective-permute-done((bf16[2,512,128]{2,1,0:T(8,128)(2,1)S(1)}, bf16[2,512,128]{2,1,0:T(8,128)(2,1)S(1)}, u32[]{:S(2)}, u32[]{:S(2)}) %collective-permute-start.3) | collective-permute-done | bytes 262176 | tf_op jit(solution)/shard_map/ppermute | solution.py:26
  45.6 3.4 %collective-permute-start.4 = (bf16[2,512,128]{2,1,0:T(8,128)(2,1)S(1)}, bf16[2,512,128]{2,1,0:T(8,128)(2,1)S(1)}, u32[]{:S(2)}, u32[]{:S(2)}) collective-permute-start(bf16[2,512,128]{2,1,0:T(8,128)(2,1)S(1)} %collective-permute-done.3.refs_0_), channel_id=1, source_target_pairs={{0,2},{1,3},{2,4},{3,5},{4,6},{5,7},{6,0},{7,1},{8,10},{9,11},{10,... | collective-permute-start | bytes 786440 | tf_op jit(solution)/shard_map/ppermute | solution.py:31
  49.0 2.4 %collective-permute-start.6 = (bf16[2,512,128]{2,1,0:T(8,128)(2,1)S(1)}, bf16[2,512,128]{2,1,0:T(8,128)(2,1)S(1)}, u32[]{:S(2)}, u32[]{:S(2)}) collective-permute-start(bf16[2,512,128]{2,1,0:T(8,128)(2,1)S(1)} %collective-permute-done.3.refs_0_), channel_id=1, source_target_pairs={{0,6},{1,7},{2,0},{3,1},{4,2},{5,3},{6,4},{7,5},{8,14},{9,15},{10,... | collective-permute-start | bytes 786440 | tf_op jit(solution)/shard_map/ppermute | solution.py:31
  51.4 4.6 %collective-permute-start.7 = (bf16[3,512,128]{2,1,0:T(8,128)(2,1)S(1)}, bf16[3,512,128]{2,1,0:T(8,128)(2,1)S(1)}, u32[]{:S(2)}, u32[]{:S(2)}) collective-permute-start(bf16[3,512,128]{2,1,0:T(8,128)(2,1)S(1)} %collective-permute-done.2.refs_0_), channel_id=1, source_target_pairs={{0,2},{1,3},{2,4},{3,5},{4,6},{5,7},{6,0},{7,1},{8,10},{9,11},{10,... | collective-permute-start | bytes 1179656 | tf_op jit(solution)/shard_map/ppermute | solution.py:31
  56.2 5.5 %shard_map.47 = (f32[2048,128]{1,0:T(8,128)S(1)}, f32[2048,128]{1,0:T(8,128)S(1)}) custom-call(s32[9]{0:T(128)S(1)} %stack.65.meta, s32[8]{0:T(128)S(1)} %reshape.7.edges, bf16[2048,128]{1,0:T(8,128)(2,1)S(1)} %copy-done, bf16[3,512,128]{2,1,0:T(8,128)(2,1)S(1)} %collective-permute-done.2.refs_0_, bf16[3,512,128]{2,1,0:T(8,128)(2,1)S(1)} %collective-permute-done.5.refs_1_, ...), custom_call_target="tpu_custom_call" | custom-call | flops 1610612736 | bytes 4194304 | tf_op jit(solution)/shard_map/pallas_call | solution.py:255
  61.7 2.1 %collective-permute-start.8 = (bf16[2,512,128]{2,1,0:T(8,128)(2,1)S(1)}, bf16[2,512,128]{2,1,0:T(8,128)(2,1)S(1)}, u32[]{:S(2)}, u32[]{:S(2)}) collective-permute-start(bf16[2,512,128]{2,1,0:T(8,128)(2,1)S(1)} %collective-permute-done.6.refs_2_), channel_id=1, source_target_pairs={{0,6},{1,7},{2,0},{3,1},{4,2},{5,3},{6,4},{7,5},{8,14},{9,15},{10,... | collective-permute-start | bytes 786440 | tf_op jit(solution)/shard_map/ppermute | solution.py:31
  63.9 3.1 %shard_map.48 = (f32[2048,128]{1,0:T(8,128)S(1)}, f32[2048,128]{1,0:T(8,128)S(1)}) custom-call(s32[9]{0:T(128)S(1)} %stack.65.meta, s32[8]{0:T(128)S(1)} %reshape.7.edges, bf16[2048,128]{1,0:T(8,128)(2,1)S(1)} %copy-done, bf16[2,512,128]{2,1,0:T(8,128)(2,1)S(1)} %collective-permute-done.3.refs_0_, bf16[2,512,128]{2,1,0:T(8,128)(2,1)S(1)} %collective-permute-done.4.refs_1_, ...), custom_call_target="tpu_custom_call" | custom-call | flops 1610612736 | bytes 4194304 | tf_op jit(solution)/shard_map/pallas_call | solution.py:255
  67.1 4.0 %collective-permute-done.8 = bf16[2,512,128]{2,1,0:T(8,128)(2,1)S(1)} collective-permute-done((bf16[2,512,128]{2,1,0:T(8,128)(2,1)S(1)}, bf16[2,512,128]{2,1,0:T(8,128)(2,1)S(1)}, u32[]{:S(2)}, u32[]{:S(2)}) %collective-permute-start.8) | collective-permute-done | bytes 262176 | tf_op jit(solution)/shard_map/ppermute | solution.py:31
  71.2 1.9 collective-permute-start.9
  73.2 4.8 %shard_map.49 = (f32[2048,128]{1,0:T(8,128)S(1)}, f32[2048,128]{1,0:T(8,128)S(1)}) custom-call(s32[9]{0:T(128)S(1)} %stack.65.meta, s32[8]{0:T(128)S(1)} %reshape.7.edges, bf16[2048,128]{1,0:T(8,128)(2,1)S(1)} %copy-done, bf16[20,512,128]{2,1,0:T(8,128)(2,1)S(1)} %constant_dynamic-update-slice_fusion.refs_0_.refs_1_, ...), custom_call_target="tpu_custom_call" | custom-call | flops 1342177280 | bytes 4194304 | tf_op jit(solution)/shard_map/pallas_call | solution.py:255
  78.1 125.8 %shard_map.50 = bf16[2048,128]{1,0:T(8,128)(2,1)} custom-call(s32[9]{0:T(128)S(1)} %stack.65.meta, s32[8]{0:T(128)S(1)} %reshape.7.edges, bf16[2048,128]{1,0:T(8,128)(2,1)S(1)} %copy-done, bf16[20,512,128]{2,1,0:T(8,128)(2,1)S(1)} %collective-permute-done.9.refs_0_, bf16[20,512,128]{2,1,0:T(8,128)(2,1)S(1)} %constant_dynamic-update-slice_fusion.refs_0_.refs_1_, ...), custom_call_target="tpu_custom_call" | custom-call | flops 5368709120 | bytes 4194304 | tf_op jit(solution)/shard_map/pallas_call | solution.py:255
  (31 shorter events, 1.3 us)
Async XLA Ops:
  0.0 0.8 copy-start.1
  0.8 0.8 copy-start.2
  1.7 29.4 %copy-start = (bf16[2048,128]{1,0:T(8,128)(2,1)S(1)}, bf16[2048,128]{1,0:T(8,128)(2,1)}, u32[]{:S(2)}) copy-start(bf16[2048,128]{1,0:T(8,128)(2,1)} %q_ref.9) | copy-start | bytes 1572868
  1.9 16.5 %collective-permute-start = (bf16[512,128]{1,0:T(8,128)(2,1)S(1)}, bf16[512,128]{1,0:T(8,128)(2,1)S(1)}, u32[]{:S(2)}, u32[]{:S(2)}) collective-permute-start(bf16[512,128]{1,0:T(8,128)(2,1)S(1)} %pack.1), channel_id=1, source_target_pairs={{0,8},{8,16},{16,24},{24,32},{32,40},{40,48},{48,56},{56,64},{64,7... | collective-permute-start | bytes 393224 | tf_op jit(solution)/shard_map/ppermute | solution.py:26
  5.7 17.1 %collective-permute-start.1 = (bf16[512,128]{1,0:T(8,128)(2,1)S(1)}, bf16[512,128]{1,0:T(8,128)(2,1)S(1)}, u32[]{:S(2)}, u32[]{:S(2)}) collective-permute-start(bf16[512,128]{1,0:T(8,128)(2,1)S(1)} %pack.1), channel_id=1, source_target_pairs={{0,16},{8,24},{16,32},{24,40},{32,48},{40,56},{48,64},{56,72},{64,... | collective-permute-start | bytes 393224 | tf_op jit(solution)/shard_map/ppermute | solution.py:26
  23.2 22.4 %collective-permute-start.2 = (bf16[3,512,128]{2,1,0:T(8,128)(2,1)S(1)}, bf16[3,512,128]{2,1,0:T(8,128)(2,1)S(1)}, u32[]{:S(2)}, u32[]{:S(2)}) collective-permute-start(bf16[3,512,128]{2,1,0:T(8,128)(2,1)S(1)} %pad_maximum_fusion.refs_0_), channel_id=1, source_target_pairs={{0,2},{1,3},{2,4},{3,5},{4,6},{5,7},{6,0},{7,1},{8,10},{9,11},{10,... | collective-permute-start | bytes 1179656 | tf_op jit(solution)/shard_map/ppermute | solution.py:31
  25.3 30.8 %collective-permute-start.5 = (bf16[3,512,128]{2,1,0:T(8,128)(2,1)S(1)}, bf16[3,512,128]{2,1,0:T(8,128)(2,1)S(1)}, u32[]{:S(2)}, u32[]{:S(2)}) collective-permute-start(bf16[3,512,128]{2,1,0:T(8,128)(2,1)S(1)} %pad_maximum_fusion.refs_0_), channel_id=1, source_target_pairs={{0,6},{1,7},{2,0},{3,1},{4,2},{5,3},{6,4},{7,5},{8,14},{9,15},{10,... | collective-permute-start | bytes 1179656 | tf_op jit(solution)/shard_map/ppermute | solution.py:31
  29.1 16.5 %collective-permute-start.3 = (bf16[2,512,128]{2,1,0:T(8,128)(2,1)S(1)}, bf16[2,512,128]{2,1,0:T(8,128)(2,1)S(1)}, u32[]{:S(2)}, u32[]{:S(2)}) collective-permute-start(bf16[2,512,128]{2,1,0:T(8,128)(2,1)S(1)} %pad_maximum_fusion.1), channel_id=1, source_target_pairs={{0,16},{8,24},{16,32},{24,40},{32,48},{40,56},{48,64},{56,72},{64,... | collective-permute-start | bytes 786440 | tf_op jit(solution)/shard_map/ppermute | solution.py:26
  45.6 18.2 %collective-permute-start.4 = (bf16[2,512,128]{2,1,0:T(8,128)(2,1)S(1)}, bf16[2,512,128]{2,1,0:T(8,128)(2,1)S(1)}, u32[]{:S(2)}, u32[]{:S(2)}) collective-permute-start(bf16[2,512,128]{2,1,0:T(8,128)(2,1)S(1)} %collective-permute-done.3.refs_0_), channel_id=1, source_target_pairs={{0,2},{1,3},{2,4},{3,5},{4,6},{5,7},{6,0},{7,1},{8,10},{9,11},{10,... | collective-permute-start | bytes 786440 | tf_op jit(solution)/shard_map/ppermute | solution.py:31
  49.0 12.7 %collective-permute-start.6 = (bf16[2,512,128]{2,1,0:T(8,128)(2,1)S(1)}, bf16[2,512,128]{2,1,0:T(8,128)(2,1)S(1)}, u32[]{:S(2)}, u32[]{:S(2)}) collective-permute-start(bf16[2,512,128]{2,1,0:T(8,128)(2,1)S(1)} %collective-permute-done.3.refs_0_), channel_id=1, source_target_pairs={{0,6},{1,7},{2,0},{3,1},{4,2},{5,3},{6,4},{7,5},{8,14},{9,15},{10,... | collective-permute-start | bytes 786440 | tf_op jit(solution)/shard_map/ppermute | solution.py:31
  51.4 15.7 %collective-permute-start.7 = (bf16[3,512,128]{2,1,0:T(8,128)(2,1)S(1)}, bf16[3,512,128]{2,1,0:T(8,128)(2,1)S(1)}, u32[]{:S(2)}, u32[]{:S(2)}) collective-permute-start(bf16[3,512,128]{2,1,0:T(8,128)(2,1)S(1)} %collective-permute-done.2.refs_0_), channel_id=1, source_target_pairs={{0,2},{1,3},{2,4},{3,5},{4,6},{5,7},{6,0},{7,1},{8,10},{9,11},{10,... | collective-permute-start | bytes 1179656 | tf_op jit(solution)/shard_map/ppermute | solution.py:31
  61.7 9.5 %collective-permute-start.8 = (bf16[2,512,128]{2,1,0:T(8,128)(2,1)S(1)}, bf16[2,512,128]{2,1,0:T(8,128)(2,1)S(1)}, u32[]{:S(2)}, u32[]{:S(2)}) collective-permute-start(bf16[2,512,128]{2,1,0:T(8,128)(2,1)S(1)} %collective-permute-done.6.refs_2_), channel_id=1, source_target_pairs={{0,6},{1,7},{2,0},{3,1},{4,2},{5,3},{6,4},{7,5},{8,14},{9,15},{10,... | collective-permute-start | bytes 786440 | tf_op jit(solution)/shard_map/ppermute | solution.py:31
  71.2 6.8 %collective-permute-start.9 = (bf16[20,512,128]{2,1,0:T(8,128)(2,1)S(1)}, bf16[20,512,128]{2,1,0:T(8,128)(2,1)S(1)}, u32[]{:S(2)}, u32[]{:S(2)}) collective-permute-start(bf16[20,512,128]{2,1,0:T(8,128)(2,1)S(1)} %constant_dynamic-update-slice_fusion.refs_0_.refs_1_), channel_id=1, source_target_pairs={{0,1},{1,0},{2,3},{3,2},{4,5},{5,4},{6,7},{7,6},{8,9},{9,8},{10,11... | collective-permute-start | bytes 7864328 | tf_op jit(solution)/shard_map/ppermute | solution.py:36
